TPU v7x, 32 devices: a whole 2x2x4 slice. The times are simulated.
32 devices in a mesh: wide: 8 (over z, y), narrow: 4 (over x, core).
Axes of the slice: x: 2, y: 2, z: 4, core: 2. Of those that a mesh axis runs over, the one named last changes fastest.
Arguments:
- frames: float32 [32768, 440], P(('wide', 'narrow')), may hold values from -8 to 8
- targets: float32 [32768, 2048], P(('wide', 'narrow')), may hold values from -7 to 7
- projection: float32 [32, 440, 512], P(('wide', 'narrow')), may hold values from -0.25 to 0.25
- phases: float32 [32, 512], P(('wide', 'narrow')), may hold values from 0 to 6.283185
- block_order: int32 [32], replicated, may hold values from 0 to 31, each once
Outputs:
- residual: float32 [32768, 2048], P(('wide', 'narrow'))
- weights: float32 [2, 512, 2048], replicated
Inputs may be any that keep to these rules, and one draw needn't show every extreme that they name: `block_order`: a permutation; steps use its first 2 entries.
All inputs are finite; a program needn't handle non-finite values.
Results may differ from a plain program's by a relative error of at most 0.0003.
Values sent between devices are 32-bit elements; how exact they have to be, the bound alone decides.
No kernel may reach another device: no remote copies, remote signals or barrier semaphores. Data moves between devices by JAX's collectives and lax.ppermute only.
A program may use at most 128 MiB of HBM per device.

v0:
```python
import jax
import jax.numpy as jnp
from jax import lax
from jax.sharding import PartitionSpec as P

STEPS = 2


def from_root(value, axis, source):
    kept = jnp.where(lax.axis_index(axis) == source, value, 0).astype(value.dtype)
    return lax.psum(kept, axis)


def features_of(frames, block_proj, block_phase):
    inner = jnp.dot(
        frames, block_proj, precision=lax.Precision.HIGHEST, preferred_element_type=jnp.float32
    )
    return jnp.sqrt(2.0 / block_proj.shape[1]) * jnp.cos(inner + block_phase[None, :])


def local_product(left, right):
    return jnp.dot(
        left.T, right, precision=lax.Precision.HIGHEST, preferred_element_type=jnp.float32
    )


def solve_block(gram_sum, cross_sum):
    width = gram_sum.shape[0]
    damping = 0.1 * jnp.trace(gram_sum) / width
    factor = jnp.linalg.cholesky(gram_sum + damping * jnp.eye(width, dtype=gram_sum.dtype))
    return jax.scipy.linalg.cho_solve((factor, True), cross_sum)


def per_device(frames, targets, projection, phases, block_order):
    feature_list = []
    for step_index in range(STEPS):
        block_proj, block_phase = (
            from_root(projection, ("wide", "narrow"), block_order[step_index]),
            from_root(phases, ("wide", "narrow"), block_order[step_index]),
        )
        feature_list.append(features_of(frames, block_proj[0], block_phase[0]))
    residual = targets
    solved = []
    for step_index in range(STEPS):
        feats = feature_list[step_index]
        cross_local = local_product(feats, residual)
        gram_sum = lax.psum(local_product(feats, feats), ("wide", "narrow"))
        cross_share = lax.psum_scatter(cross_local, "narrow", scatter_dimension=1, tiled=True)
        cross_share = lax.psum(cross_share, "wide")
        weight_share = solve_block(gram_sum, cross_share)
        weights = lax.all_gather(weight_share, "narrow", axis=1, tiled=True)
        residual = residual - jnp.dot(
            feats, weights, precision=lax.Precision.HIGHEST, preferred_element_type=jnp.float32
        )
        solved.append(weights)
    return (residual, jnp.stack(solved))


def solution(mesh):
    return jax.shard_map(
        per_device,
        mesh=mesh,
        in_specs=(
            P(("wide", "narrow"), None),
            P(("wide", "narrow"), None),
            P(("wide", "narrow"), None, None),
            P(("wide", "narrow"), None),
            P(),
        ),
        out_specs=(P(("wide", "narrow"), None), P()),
        check_vma=False,
    )
```

profile of v0, /device:TPU:0, one launch (start us, length us, event | category | flops | bytes accessed | tf_op | source)
XLA Modules:
  0.0 830.9 jit_solution(9541933310264790107)
XLA Ops:
  12.6 42.1 %all-reduce.1 = (f32[512]{0:T(512)S(1)}, f32[512]{0:T(512)S(1)}) all-reduce(f32[512]{0:T(512)S(1)} %bitcast.143, f32[512]{0:T(512)S(1)} %bitcast.142), channel_id=1, replica_groups=mesh['wide'=8,'narrow'=4] {'wide','narrow'}, use_global_device_ids=true, to_apply=%region_1.2 | all-reduce | flops 1024 | bytes 8192 | tf_op jit(solution)/shard_map/psum | solution.py:11
  54.7 96.0 %all-reduce.15.cloned.1.call-done = (f32[440,512]{1,0:T(8,128)}, f32[440,512]{1,0:T(8,128)}) async-done(((f32[440,512]{1,0:T(8,128)}, f32[440,512]{1,0:T(8,128)}), (f32[440,512]{1,0:T(8,128)}, f32[440,512]{1,0:T(8,128)})) %all-reduce.15.cloned.1.call-update) | async-done | bytes 1802256 | tf_op jit(solution)/shard_map/psum | solution.py:11
  150.7 11.2 %cosine_multiply_fusion.1 = f32[512,1024]{1,0:T(8,128)S(1)} fusion(f32[440,512]{1,0:T(8,128)} %get-tuple-element.40, f32[1024,440]{0,1:T(8,128)S(1)} %copy-done, f32[512]{0:T(512)S(1)} %get-tuple-element.36), kind=kOutput, calls=%fused_computation.8 | convolution fusion | flops 2769289216 | bytes 4802560 | tf_op jit(solution)/shard_map/dot_general | solution.py:15
  162.0 13.4 %fusion.97 = f32[512,512]{0,1:T(8,128)} fusion(f32[512,1024]{1,0:T(8,128)S(1)} %cosine_multiply_fusion.1), kind=kOutput, calls=%fused_computation.185 | convolution fusion | flops 3221225472 | bytes 3145728 | tf_op jit(solution)/shard_map/dot_general | solution.py:22
  175.3 10.3 %cosine_multiply_fusion = f32[512,1024]{1,0:T(8,128)S(1)} fusion(f32[440,512]{1,0:T(8,128)S(1)} %copy-done.11, f32[1024,440]{0,1:T(8,128)S(1)} %copy-done, f32[512]{0:T(512)S(1)} %get-tuple-element.37), kind=kOutput, calls=%fused_computation.7 | convolution fusion | flops 2769289216 | bytes 4802560 | tf_op jit(solution)/shard_map/dot_general | solution.py:15
  191.7 18.0 %fusion.98 = f32[512,2048]{1,0:T(8,128)} fusion(f32[512,1024]{1,0:T(8,128)} %copy-done.5, f32[1024,2048]{1,0:T(8,128)} %param.9), kind=kOutput, calls=%fused_computation.186 | convolution fusion | flops 12884901888 | bytes 14680064 | tf_op jit(solution)/shard_map/dot_general | solution.py:22
  210.2 115.3 %all-reduce.13.cloned.1.call-done = (f32[512,512]{0,1:T(8,128)}, f32[512,512]{0,1:T(8,128)}) async-done(((f32[512,512]{0,1:T(8,128)}, f32[512,512]{0,1:T(8,128)}), (f32[512,512]{0,1:T(8,128)}, f32[512,512]{0,1:T(8,128)})) %all-reduce.13.cloned.1.call-update) | async-done | bytes 2097168 | tf_op jit(solution)/shard_map/psum | solution.py:47
  336.4 11.7 %cholesky.286 = f32[128,128]{1,0:T(8,128)S(1)} custom-call(f32[128,128]{1,0:T(8,128)S(1)} %cholesky.426), custom_call_target="Cholesky" | custom-call | tf_op jit(solution)/shard_map/jit(cholesky)/cholesky | solution.py:30
  348.2 9.8 %custom-call.29 = f32[1,128,128]{1,2,0:T(8,128)S(1)} custom-call(f32[1,128,128]{2,1,0:T(8,128)S(1)} %get-tuple-element.67), custom_call_target="InvertDiagBlocksLowerTriangular" | custom-call | tf_op jit(solution)/shard_map/jit(cholesky)/cholesky | solution.py:30
  360.6 11.7 %cholesky.305 = f32[128,128]{1,0:T(8,128)S(1)} custom-call(f32[128,128]{1,0:T(8,128)S(1)} %cholesky.430), custom_call_target="Cholesky" | custom-call | tf_op jit(solution)/shard_map/jit(cholesky)/cholesky | solution.py:30
  372.4 10.0 %custom-call.30 = f32[1,128,128]{1,2,0:T(8,128)S(1)} custom-call(f32[1,128,128]{2,1,0:T(8,128)S(1)} %get-tuple-element.64), custom_call_target="InvertDiagBlocksLowerTriangular" | custom-call | tf_op jit(solution)/shard_map/jit(cholesky)/cholesky | solution.py:30
  383.9 11.7 %cholesky.326 = f32[128,128]{1,0:T(8,128)S(1)} custom-call(f32[128,128]{1,0:T(8,128)S(1)} %cholesky.435), custom_call_target="Cholesky" | custom-call | tf_op jit(solution)/shard_map/jit(cholesky)/cholesky | solution.py:30
  395.7 9.8 %custom-call.31 = f32[1,128,128]{1,2,0:T(8,128)S(1)} custom-call(f32[1,128,128]{2,1,0:T(8,128)S(1)} %get-tuple-element.61), custom_call_target="InvertDiagBlocksLowerTriangular" | custom-call | tf_op jit(solution)/shard_map/jit(cholesky)/cholesky | solution.py:30
  406.9 11.9 %cholesky.343 = f32[128,128]{1,0:T(8,128)S(1)} custom-call(f32[128,128]{1,0:T(8,128)S(1)} %convolution_subtract_fusion.19), custom_call_target="Cholesky" | custom-call | tf_op jit(solution)/shard_map/jit(cholesky)/cholesky | solution.py:30
  425.5 11.8 %while.4 = (s32[]{:T(128)}, f32[512,512]{1,0:T(8,128)}, s32[4,2]{0,1:T(2,128)S(1)}, f32[4,128,128]{2,1,0:T(8,128)S(1)}, s32[]{:T(128)}) while((s32[]{:T(128)}, f32[512,512]{1,0:T(8,128)}, s32[4,2]{0,1:T(2,128)S(1)}, f32[4,128,128]{2,1,0:T(8,128)S(1)}, s32[]{:T(128)}) %tuple.58), condition=%wide.while_cond, body=%wide.while_body.sunk | while | flops 2 | bytes 131189 | solution.py:31
  437.3 39.3 %custom-call.32 = f32[4,128,128]{1,2,0:T(8,128)S(1)} custom-call(f32[4,128,128]{2,1,0:T(8,128)S(1)} %get-tuple-element.18), custom_call_target="InvertDiagBlocksLowerTriangular" | custom-call | tf_op jit(solution)/shard_map/jit(_cho_solve)/triangular_solve | solution.py:31
  476.6 26.8 %all-reduce.9.cloned.1.call-done = f32[512,512]{1,0:T(8,128)} async-done(((f32[512,512]{1,0:T(8,128)}), f32[512,512]{1,0:T(8,128)}) %all-reduce.9.cloned.1.call-update) | async-done | bytes 1048592 | tf_op jit(solution)/shard_map/psum | solution.py:49
  515.0 33.7 %all-gather.3.cloned.1.call-done = f32[512,2048]{1,0:T(8,128)} async-done(((f32[512,512]{1,0:T(8,128)}), f32[512,2048]{1,0:T(8,128)}) %all-gather.3.cloned.1.call-update) | async-done | bytes 4194320 | tf_op jit(solution)/shard_map/all_gather | solution.py:51
  548.8 16.9 %convolution_subtract_fusion.1 = f32[1024,2048]{1,0:T(8,128)S(1)} fusion(f32[1024,2048]{1,0:T(8,128)} %param.9, f32[512,1024]{1,0:T(8,128)} %copy-done.5, f32[512,2048]{1,0:T(8,128)} %all-gather.3.cloned.1.call-done), kind=kOutput, calls=%fused_computation.6 | convolution fusion | flops 12886999040 | bytes 23068672 | tf_op jit(solution)/shard_map/dot_general | solution.py:52
  569.1 17.2 %fusion.100 = f32[512,2048]{1,0:T(8,128)} fusion(f32[512,1024]{1,0:T(8,128)} %copy-done.3, f32[1024,2048]{1,0:T(8,128)S(1)} %convolution_subtract_fusion.1), kind=kOutput, calls=%fused_computation.188 | convolution fusion | flops 12884901888 | bytes 14680064 | tf_op jit(solution)/shard_map/dot_general | solution.py:22
  588.1 11.7 %cholesky.358 = f32[128,128]{1,0:T(8,128)S(1)} custom-call(f32[128,128]{1,0:T(8,128)S(1)} %cholesky.439), custom_call_target="Cholesky" | custom-call | tf_op jit(solution)/shard_map/jit(cholesky)/cholesky | solution.py:30
  599.9 9.8 %custom-call.33 = f32[1,128,128]{1,2,0:T(8,128)S(1)} custom-call(f32[1,128,128]{2,1,0:T(8,128)S(1)} %get-tuple-element.57), custom_call_target="InvertDiagBlocksLowerTriangular" | custom-call | tf_op jit(solution)/shard_map/jit(cholesky)/cholesky | solution.py:30
  612.3 11.7 %cholesky.377 = f32[128,128]{1,0:T(8,128)S(1)} custom-call(f32[128,128]{1,0:T(8,128)S(1)} %cholesky.443), custom_call_target="Cholesky" | custom-call | tf_op jit(solution)/shard_map/jit(cholesky)/cholesky | solution.py:30
  624.1 10.0 %custom-call.34 = f32[1,128,128]{1,2,0:T(8,128)S(1)} custom-call(f32[1,128,128]{2,1,0:T(8,128)S(1)} %get-tuple-element.54), custom_call_target="InvertDiagBlocksLowerTriangular" | custom-call | tf_op jit(solution)/shard_map/jit(cholesky)/cholesky | solution.py:30
  635.7 11.7 %cholesky.398 = f32[128,128]{1,0:T(8,128)S(1)} custom-call(f32[128,128]{1,0:T(8,128)S(1)} %cholesky.448), custom_call_target="Cholesky" | custom-call | tf_op jit(solution)/shard_map/jit(cholesky)/cholesky | solution.py:30
  647.4 9.8 %custom-call.35 = f32[1,128,128]{1,2,0:T(8,128)S(1)} custom-call(f32[1,128,128]{2,1,0:T(8,128)S(1)} %get-tuple-element.51), custom_call_target="InvertDiagBlocksLowerTriangular" | custom-call | tf_op jit(solution)/shard_map/jit(cholesky)/cholesky | solution.py:30
  658.7 11.7 %cholesky.415 = f32[128,128]{1,0:T(8,128)S(1)} custom-call(f32[128,128]{1,0:T(8,128)S(1)} %convolution_subtract_fusion.18), custom_call_target="Cholesky" | custom-call | tf_op jit(solution)/shard_map/jit(cholesky)/cholesky | solution.py:30
  684.2 39.3 %custom-call.36 = f32[4,128,128]{1,2,0:T(8,128)S(1)} custom-call(f32[4,128,128]{2,1,0:T(8,128)S(1)} %get-tuple-element.19), custom_call_target="InvertDiagBlocksLowerTriangular" | custom-call | tf_op jit(solution)/shard_map/jit(_cho_solve)/triangular_solve | solution.py:31
  723.5 31.3 %all-reduce.11.cloned.1.call-done = f32[512,512]{1,0:T(8,128)} async-done(((f32[512,512]{1,0:T(8,128)}), f32[512,512]{1,0:T(8,128)}) %all-reduce.11.cloned.1.call-update) | async-done | bytes 1048592 | tf_op jit(solution)/shard_map/psum | solution.py:49
  764.2 34.2 %all-gather.5.cloned.1.call-done = f32[512,2048]{1,0:T(8,128)} async-done(((f32[512,512]{1,0:T(8,128)}), f32[512,2048]{1,0:T(8,128)}) %all-gather.5.cloned.1.call-update) | async-done | bytes 4194320 | tf_op jit(solution)/shard_map/all_gather | solution.py:51
  798.4 8.1 pad_maximum_fusion
  806.5 17.1 %convolution_subtract_fusion = f32[1024,2048]{1,0:T(8,128)} fusion(f32[1024,2048]{1,0:T(8,128)} %copy-done.2, f32[512,1024]{1,0:T(8,128)S(1)} %copy-done.4, f32[512,2048]{1,0:T(8,128)S(1)} %copy-done.6), kind=kOutput, calls=%fused_computation.5 | convolution fusion | flops 12886999040 | bytes 23068672 | tf_op jit(solution)/shard_map/dot_general | solution.py:52
  (152 shorter events, 92.4 us)
Async XLA Ops:
  7.2 143.5 %copy-start = (f32[1024,440]{0,1:T(8,128)S(1)}, f32[1024,440]{0,1:T(8,128)}, u32[]{:S(2)}) copy-start(f32[1024,440]{0,1:T(8,128)} %param.8) | copy-start | bytes 5406724
  7.2 143.5 %all-reduce.15.cloned.1.call-start = ((), (), s32[]{:S(2)}) async-start(), calls=%async_computation.9 | async-start | bytes 3604480 | tf_op jit(solution)/shard_map/psum | solution.py:11
  9.9 2.7 copy-start.12
  12.6 312.9 %all-reduce.13.cloned.1.call-start = ((), (), s32[]{:S(2)}) async-start(), calls=%async_computation.8 | async-start | bytes 4194304 | tf_op jit(solution)/shard_map/psum | solution.py:47
  161.9 13.4 %copy-start.5 = (f32[512,1024]{1,0:T(8,128)}, f32[512,1024]{1,0:T(8,128)S(1)}, u32[]{:S(2)}) copy-start(f32[512,1024]{1,0:T(8,128)S(1)} %cosine_multiply_fusion.1) | copy-start | bytes 6291460
  162.0 13.4 %copy-start.11 = (f32[440,512]{1,0:T(8,128)S(1)}, f32[440,512]{1,0:T(8,128)}, u32[]{:S(2)}) copy-start(f32[440,512]{1,0:T(8,128)} %get-tuple-element.41) | copy-start | bytes 2703364
  185.7 1.4 copy-start.3
  191.6 233.8 %reduce-scatter.3.cloned.1.call-start = ((), (), s32[]{:S(2)}) async-start(), calls=%async_computation.2 | async-start | bytes 5242880 | tf_op jit(solution)/shard_map/reduce_scatter | solution.py:48
  209.7 293.7 %all-reduce.9.cloned.1.call-start = ((), (), s32[]{:S(2)}) async-start(), calls=%async_computation.3 | async-start | bytes 2097152 | tf_op jit(solution)/shard_map/psum | solution.py:49
  335.4 1.0 copy-start.8
  425.4 123.4 %all-gather.3.cloned.1.call-start = ((), (), s32[]{:S(2)}) async-start(), calls=%async_computation.4 | async-start | bytes 5242880 | tf_op jit(solution)/shard_map/all_gather | solution.py:51
  437.3 69.3 %copy-start.7 = (f32[512,512]{1,0:T(8,128)S(1)}, f32[512,512]{1,0:T(8,128)}, u32[]{:S(2)}) copy-start(f32[512,512]{1,0:T(8,128)} %get-tuple-element.187) | copy-start | bytes 3145732
  514.6 161.5 %reduce-scatter.5.cloned.1.call-start = ((), (), s32[]{:S(2)}) async-start(), calls=%async_computation.5 | async-start | bytes 5242880 | tf_op jit(solution)/shard_map/reduce_scatter | solution.py:48
  565.7 3.4 copy-start.2
  586.3 168.6 %all-reduce.11.cloned.1.call-start = ((), (), s32[]{:S(2)}) async-start(), calls=%async_computation.6 | async-start | bytes 2097152 | tf_op jit(solution)/shard_map/psum | solution.py:49
  587.1 1.0 copy-start.9
  676.1 122.3 %all-gather.5.cloned.1.call-start = ((), (), s32[]{:S(2)}) async-start(), calls=%async_computation.7 | async-start | bytes 5242880 | tf_op jit(solution)/shard_map/all_gather | solution.py:51
  754.9 3.2 copy-start.10
  798.4 8.1 copy-start.4
  798.4 8.1 copy-start.6
  806.5 17.2 %copy-start.1 = (f32[1024,440]{0,1:T(8,128)S(1)}, f32[1024,440]{0,1:T(8,128)}, u32[]{:S(2)}) copy-start(f32[1024,440]{0,1:T(8,128)} %param.8) | copy-start | bytes 5406724
Sparse Core Ops, SparseCore 0:
  14.0 136.6 all-reduce.14
  191.7 133.7 all-reduce.12
  328.6 43.2 reduce-scatter.2
  425.5 77.8 all-reduce.8
  514.7 34.0 all-gather.2
  586.4 44.4 reduce-scatter.4
  676.2 78.6 all-reduce.10
  764.3 34.0 all-gather.4
where the time goes:
time: 841 us; the launch traced here: 831 us
  waiting for transfers between devices  338 us (40%)
  other arithmetic  259 us (31%)
  matrix products  138 us (16%)
  blocking collectives  42.1 us (5%)
  local copies, waits for them, and re-layouts  29.9 us (4%)
  between operations  23 us (3%)
    another operation x30, other arithmetic, solve_block(): jnp.linalg.cholesky(gram_sum + damping * jnp.eye(width, dtype=gram_sum.dt...  159 us
    psum x1, waiting for transfers between devices, per_device(): gram_sum = lax.psum(local_product(feats, feats), ('wide', 'narrow'))  115 us
    psum x1, waiting for transfers between devices, from_root(): return lax.psum(kept, axis)  96 us
    another operation x7, other arithmetic, solve_block(): return jax.scipy.linalg.cho_solve((factor, True), cross_sum)  82.2 us
    all_gather x2, waiting for transfers between devices, per_device(): weights = lax.all_gather(weight_share, 'narrow', axis=1, tiled=True)  68 us
    psum x2, waiting for transfers between devices, per_device(): cross_share = lax.psum(cross_share, 'wide')  58.2 us
    dot_general x4, matrix products, local_product(): jnp.dot(left.T, right, precision=lax.Precision.HIGHEST, preferred_element...  53.1 us
    psum x1, blocking collectives, from_root(): return lax.psum(kept, axis)  42.1 us
  transfers between devices with their start and end apart: 8, of which 6 were waited for; matrix products, arithmetic and copies ran while one was open for 36% of the time, Pallas kernels for 0%

commit v1 on v0

--- a/solution.py
+++ b/solution.py
@@ -44,7 +44,7 @@
     for step_index in range(STEPS):
         feats = feature_list[step_index]
         cross_local = local_product(feats, residual)
-        gram_sum = lax.psum(local_product(feats, feats), ("wide", "narrow"))
+        gram_sum = lax.psum(lax.psum(local_product(feats, feats), "narrow"), "wide")
         cross_share = lax.psum_scatter(cross_local, "narrow", scatter_dimension=1, tiled=True)
         cross_share = lax.psum(cross_share, "wide")
         weight_share = solve_block(gram_sum, cross_share)

time: 841 us -> 993 us (1.18)
  waiting for transfers between devices: 338 us -> 499 us
    psum x2, waiting for transfers between devices: 58.2 us -> 211 us  [per_device(): cross_share = lax.psum(cross_share, 'wide')]
    reduce_scatter x2, waiting for transfers between devices: 0.02 us -> 92.2 us  [per_device(): lax.psum_scatter(cross_local, 'narrow', scatter_dimension=1, tiled=True)]
    psum x1, waiting for transfers between devices: 115 us -> 32.6 us  [per_device(): gram_sum = lax.psum(lax.psum(local_product(feats, feats), 'narrow'), 'wide')]
    another operation x30 -> x29, other arithmetic: 159 us -> 158 us  [solve_block(): jnp.linalg.cholesky(gram_sum + damping * jnp.eye(width, dtype=gram_sum.dt...]
  transfers between devices with their start and end apart: 8 -> 8, of which waited for: 6 -> 8; matrix products, arithmetic and copies ran while one was open for 36% -> 2% of each run, Pallas kernels for 0% -> 0%
where the time goes in v1:
time: 993 us; the launch traced here: 983 us
  waiting for transfers between devices  499 us (50%)
  other arithmetic  260 us (26%)
  matrix products  132 us (13%)
  blocking collectives  42.1 us (4%)
  local copies, waits for them, and re-layouts  25.3 us (3%)
  between operations  22.9 us (2%)
    psum x2, waiting for transfers between devices, per_device(): cross_share = lax.psum(cross_share, 'wide')  211 us
    another operation x29, other arithmetic, solve_block(): jnp.linalg.cholesky(gram_sum + damping * jnp.eye(width, dtype=gram_sum.dt...  158 us
    psum x1, waiting for transfers between devices, from_root(): return lax.psum(kept, axis)  95.9 us
    reduce_scatter x2, waiting for transfers between devices, per_device(): lax.psum_scatter(cross_local, 'narrow', scatter_dimension=1, tiled=True)  92.2 us
    another operation x7, other arithmetic, solve_block(): return jax.scipy.linalg.cho_solve((factor, True), cross_sum)  81 us
    all_gather x2, waiting for transfers between devices, per_device(): weights = lax.all_gather(weight_share, 'narrow', axis=1, tiled=True)  67.4 us
    dot_general x4, matrix products, local_product(): jnp.dot(left.T, right, precision=lax.Precision.HIGHEST, preferred_element...  53.2 us
    psum x1, blocking collectives, from_root(): return lax.psum(kept, axis)  42.1 us
  transfers between devices with their start and end apart: 8, of which 8 were waited for; matrix products, arithmetic and copies ran while one was open for 2% of the time, Pallas kernels for 0%

profile of v1, /device:TPU:0, one launch (start us, length us, event | category | flops | bytes accessed | tf_op | source)
XLA Modules:
  0.0 983.0 jit_solution(13588131492743810394)
XLA Ops:
  12.6 42.1 %all-reduce.1 = (f32[512]{0:T(512)S(1)}, f32[512]{0:T(512)S(1)}) all-reduce(f32[512]{0:T(512)S(1)} %bitcast.143, f32[512]{0:T(512)S(1)} %bitcast.142), channel_id=1, replica_groups=mesh['wide'=8,'narrow'=4] {'wide','narrow'}, use_global_device_ids=true, to_apply=%region_1.2 | all-reduce | flops 1024 | bytes 8192 | tf_op jit(solution)/shard_map/psum | solution.py:11
  54.8 95.9 %all-reduce.11.cloned.1.call-done = (f32[440,512]{1,0:T(8,128)}, f32[440,512]{1,0:T(8,128)}) async-done(((f32[440,512]{1,0:T(8,128)}, f32[440,512]{1,0:T(8,128)}), (f32[440,512]{1,0:T(8,128)}, f32[440,512]{1,0:T(8,128)})) %all-reduce.11.cloned.1.call-update) | async-done | bytes 1802256 | tf_op jit(solution)/shard_map/psum | solution.py:11
  150.7 11.2 %cosine_multiply_fusion.1 = f32[512,1024]{1,0:T(8,128)S(1)} fusion(f32[440,512]{1,0:T(8,128)} %get-tuple-element.38, f32[1024,440]{0,1:T(8,128)S(1)} %copy-done, f32[512]{0:T(512)S(1)} %get-tuple-element.36), kind=kOutput, calls=%fused_computation.8 | convolution fusion | flops 2769289216 | bytes 4802560 | tf_op jit(solution)/shard_map/dot_general | solution.py:15
  162.0 13.4 %fusion.97 = f32[512,512]{0,1:T(8,128)} fusion(f32[512,1024]{1,0:T(8,128)S(1)} %cosine_multiply_fusion.1), kind=kOutput, calls=%fused_computation.185 | convolution fusion | flops 3221225472 | bytes 3145728 | tf_op jit(solution)/shard_map/dot_general | solution.py:22
  175.4 10.3 %cosine_multiply_fusion = f32[512,1024]{1,0:T(8,128)S(1)} fusion(f32[440,512]{1,0:T(8,128)S(1)} %copy-done.9, f32[1024,440]{0,1:T(8,128)S(1)} %copy-done, f32[512]{0:T(512)S(1)} %get-tuple-element.37), kind=kOutput, calls=%fused_computation.7 | convolution fusion | flops 2769289216 | bytes 4802560 | tf_op jit(solution)/shard_map/dot_general | solution.py:15
  191.7 18.0 %fusion.98 = f32[512,2048]{1,0:T(8,128)} fusion(f32[512,1024]{1,0:T(8,128)} %copy-done.5, f32[1024,2048]{1,0:T(8,128)} %param.9), kind=kOutput, calls=%fused_computation.186 | convolution fusion | flops 12884901888 | bytes 14680064 | tf_op jit(solution)/shard_map/dot_general | solution.py:22
  209.8 32.6 %all-reduce.17.cloned.1.call-done = (f32[512,512]{0,1:T(8,128)}, f32[512,512]{0,1:T(8,128)}) async-done(((f32[512,512]{0,1:T(8,128)}, f32[512,512]{0,1:T(8,128)}), (f32[512,512]{0,1:T(8,128)}, f32[512,512]{0,1:T(8,128)})) %all-reduce.17.cloned.1.call-update) | async-done | bytes 2097168 | tf_op jit(solution)/shard_map/psum | solution.py:47
  242.4 47.6 %reduce-scatter.3.cloned.1.call-done = f32[512,512]{1,0:T(8,128)} async-done(((f32[512,2048]{1,0:T(8,128)}), f32[512,512]{1,0:T(8,128)}) %reduce-scatter.3.cloned.1.call-update) | async-done | bytes 1048592 | tf_op jit(solution)/shard_map/reduce_scatter | solution.py:48
  290.5 105.4 %all-reduce.15.cloned.1.call-done = (f32[512,512]{1,0:T(8,128)}, f32[512,512]{0,1:T(8,128)}) async-done(((f32[512,512]{1,0:T(8,128)}, f32[512,512]{0,1:T(8,128)}), (f32[512,512]{1,0:T(8,128)}, f32[512,512]{0,1:T(8,128)})) %all-reduce.15.cloned.1.call-update) | async-done | bytes 2097168 | tf_op jit(solution)/shard_map/psum | solution.py:49
  402.6 11.7 %cholesky.286 = f32[128,128]{1,0:T(8,128)S(1)} custom-call(f32[128,128]{1,0:T(8,128)S(1)} %cholesky.426), custom_call_target="Cholesky" | custom-call | tf_op jit(solution)/shard_map/jit(cholesky)/cholesky | solution.py:30
  414.4 9.8 custom-call.29
  425.0 11.7 %cholesky.305 = f32[128,128]{1,0:T(8,128)S(1)} custom-call(f32[128,128]{1,0:T(8,128)S(1)} %cholesky.430), custom_call_target="Cholesky" | custom-call | tf_op jit(solution)/shard_map/jit(cholesky)/cholesky | solution.py:30
  436.7 10.0 %custom-call.30 = f32[1,128,128]{1,2,0:T(8,128)S(1)} custom-call(f32[1,128,128]{2,1,0:T(8,128)S(1)} %get-tuple-element.68), custom_call_target="InvertDiagBlocksLowerTriangular" | custom-call | tf_op jit(solution)/shard_map/jit(cholesky)/cholesky | solution.py:30
  447.4 11.7 %cholesky.326 = f32[128,128]{1,0:T(8,128)S(1)} custom-call(f32[128,128]{1,0:T(8,128)S(1)} %cholesky.435), custom_call_target="Cholesky" | custom-call | tf_op jit(solution)/shard_map/jit(cholesky)/cholesky | solution.py:30
  459.9 9.8 custom-call.31
  470.3 11.7 %cholesky.343 = f32[128,128]{1,0:T(8,128)S(1)} custom-call(f32[128,128]{1,0:T(8,128)S(1)} %convolution_subtract_fusion.19), custom_call_target="Cholesky" | custom-call | tf_op jit(solution)/shard_map/jit(cholesky)/cholesky | solution.py:30
  494.7 39.3 %custom-call.32 = f32[4,128,128]{1,2,0:T(8,128)S(1)} custom-call(f32[4,128,128]{2,1,0:T(8,128)S(1)} %get-tuple-element.18), custom_call_target="InvertDiagBlocksLowerTriangular" | custom-call | tf_op jit(solution)/shard_map/jit(_cho_solve)/triangular_solve | solution.py:31
  545.6 33.4 %all-gather.3.cloned.1.call-done = f32[512,2048]{1,0:T(8,128)} async-done(((f32[512,512]{1,0:T(8,128)}), f32[512,2048]{1,0:T(8,128)}) %all-gather.3.cloned.1.call-update) | async-done | bytes 4194320 | tf_op jit(solution)/shard_map/all_gather | solution.py:51
  579.0 16.9 %convolution_subtract_fusion.1 = f32[1024,2048]{1,0:T(8,128)S(1)} fusion(f32[1024,2048]{1,0:T(8,128)} %param.9, f32[512,1024]{1,0:T(8,128)} %copy-done.5, f32[512,2048]{1,0:T(8,128)} %all-gather.3.cloned.1.call-done), kind=kOutput, calls=%fused_computation.6 | convolution fusion | flops 12886999040 | bytes 23068672 | tf_op jit(solution)/shard_map/dot_general | solution.py:52
  599.3 17.2 %fusion.100 = f32[512,2048]{1,0:T(8,128)} fusion(f32[512,1024]{1,0:T(8,128)} %copy-done.3, f32[1024,2048]{1,0:T(8,128)S(1)} %convolution_subtract_fusion.1), kind=kOutput, calls=%fused_computation.188 | convolution fusion | flops 12884901888 | bytes 14680064 | tf_op jit(solution)/shard_map/dot_general | solution.py:22
  616.6 44.5 %reduce-scatter.5.cloned.1.call-done = f32[512,512]{1,0:T(8,128)} async-done(((f32[512,2048]{1,0:T(8,128)}), f32[512,512]{1,0:T(8,128)}) %reduce-scatter.5.cloned.1.call-update) | async-done | bytes 1048592 | tf_op jit(solution)/shard_map/reduce_scatter | solution.py:48
  661.4 105.8 %all-reduce.13.cloned.1.call-done = (f32[512,512]{1,0:T(8,128)}, f32[512,512]{0,1:T(8,128)}) async-done(((f32[512,512]{1,0:T(8,128)}, f32[512,512]{0,1:T(8,128)}), (f32[512,512]{1,0:T(8,128)}, f32[512,512]{0,1:T(8,128)})) %all-reduce.13.cloned.1.call-update) | async-done | bytes 2097168 | tf_op jit(solution)/shard_map/psum | solution.py:49
  773.9 11.7 %cholesky.358 = f32[128,128]{1,0:T(8,128)S(1)} custom-call(f32[128,128]{1,0:T(8,128)S(1)} %cholesky.439), custom_call_target="Cholesky" | custom-call | tf_op jit(solution)/shard_map/jit(cholesky)/cholesky | solution.py:30
  786.3 9.8 custom-call.33
  796.9 11.7 %cholesky.377 = f32[128,128]{1,0:T(8,128)S(1)} custom-call(f32[128,128]{1,0:T(8,128)S(1)} %cholesky.443), custom_call_target="Cholesky" | custom-call | tf_op jit(solution)/shard_map/jit(cholesky)/cholesky | solution.py:30
  809.3 10.0 %custom-call.34 = f32[1,128,128]{1,2,0:T(8,128)S(1)} custom-call(f32[1,128,128]{2,1,0:T(8,128)S(1)} %get-tuple-element.58), custom_call_target="InvertDiagBlocksLowerTriangular" | custom-call | tf_op jit(solution)/shard_map/jit(cholesky)/cholesky | solution.py:30
  820.0 11.7 %cholesky.398 = f32[128,128]{1,0:T(8,128)S(1)} custom-call(f32[128,128]{1,0:T(8,128)S(1)} %cholesky.448), custom_call_target="Cholesky" | custom-call | tf_op jit(solution)/shard_map/jit(cholesky)/cholesky | solution.py:30
  832.4 9.8 custom-call.35
  842.8 11.9 %cholesky.415 = f32[128,128]{1,0:T(8,128)S(1)} custom-call(f32[128,128]{1,0:T(8,128)S(1)} %convolution_subtract_fusion.18), custom_call_target="Cholesky" | custom-call | tf_op jit(solution)/shard_map/jit(cholesky)/cholesky | solution.py:30
  866.1 39.3 %custom-call.36 = f32[4,128,128]{1,2,0:T(8,128)S(1)} custom-call(f32[4,128,128]{2,1,0:T(8,128)S(1)} %get-tuple-element.19), custom_call_target="InvertDiagBlocksLowerTriangular" | custom-call | tf_op jit(solution)/shard_map/jit(_cho_solve)/triangular_solve | solution.py:31
  916.5 33.9 %all-gather.5.cloned.1.call-done = f32[512,2048]{1,0:T(8,128)} async-done(((f32[512,512]{1,0:T(8,128)}), f32[512,2048]{1,0:T(8,128)}) %all-gather.5.cloned.1.call-update) | async-done | bytes 4194320 | tf_op jit(solution)/shard_map/all_gather | solution.py:51
  958.6 17.1 %convolution_subtract_fusion = f32[1024,2048]{1,0:T(8,128)} fusion(f32[1024,2048]{1,0:T(8,128)} %copy-done.2, f32[512,1024]{1,0:T(8,128)S(1)} %copy-done.4, f32[512,2048]{1,0:T(8,128)S(1)} %copy-done.6), kind=kOutput, calls=%fused_computation.5 | convolution fusion | flops 12886999040 | bytes 23068672 | tf_op jit(solution)/shard_map/dot_general | solution.py:52
  (148 shorter events, 99.1 us)
Async XLA Ops:
  7.2 143.5 %copy-start = (f32[1024,440]{0,1:T(8,128)S(1)}, f32[1024,440]{0,1:T(8,128)}, u32[]{:S(2)}) copy-start(f32[1024,440]{0,1:T(8,128)} %param.8) | copy-start | bytes 5406724
  7.2 143.5 %all-reduce.11.cloned.1.call-start = ((), (), s32[]{:S(2)}) async-start(), calls=%async_computation.6 | async-start | bytes 3604480 | tf_op jit(solution)/shard_map/psum | solution.py:11
  9.9 2.7 copy-start.10
  12.6 229.8 %all-reduce.17.cloned.1.call-start = ((), (), s32[]{:S(2)}) async-start(), calls=%async_computation.9 | async-start | bytes 4194304 | tf_op jit(solution)/shard_map/psum | solution.py:47
  161.9 13.4 %copy-start.5 = (f32[512,1024]{1,0:T(8,128)}, f32[512,1024]{1,0:T(8,128)S(1)}, u32[]{:S(2)}) copy-start(f32[512,1024]{1,0:T(8,128)S(1)} %cosine_multiply_fusion.1) | copy-start | bytes 6291460
  162.0 13.4 %copy-start.9 = (f32[440,512]{1,0:T(8,128)S(1)}, f32[440,512]{1,0:T(8,128)}, u32[]{:S(2)}) copy-start(f32[440,512]{1,0:T(8,128)} %get-tuple-element.39) | copy-start | bytes 2703364
  185.7 1.4 copy-start.3
  191.7 98.3 %reduce-scatter.3.cloned.1.call-start = ((), (), s32[]{:S(2)}) async-start(), calls=%async_computation.2 | async-start | bytes 5242880 | tf_op jit(solution)/shard_map/reduce_scatter | solution.py:48
  209.7 186.1 %all-reduce.15.cloned.1.call-start = ((), (), s32[]{:S(2)}) async-start(), calls=%async_computation.8 | async-start | bytes 4194304 | tf_op jit(solution)/shard_map/psum | solution.py:49
  290.0 289.0 %all-gather.3.cloned.1.call-start = ((), (), s32[]{:S(2)}) async-start(), calls=%async_computation.3 | async-start | bytes 5242880 | tf_op jit(solution)/shard_map/all_gather | solution.py:51
  398.4 2.7 copy-start.7
  545.1 116.0 %reduce-scatter.5.cloned.1.call-start = ((), (), s32[]{:S(2)}) async-start(), calls=%async_computation.4 | async-start | bytes 5242880 | tf_op jit(solution)/shard_map/reduce_scatter | solution.py:48
  595.9 3.4 copy-start.2
  616.5 150.6 %all-reduce.13.cloned.1.call-start = ((), (), s32[]{:S(2)}) async-start(), calls=%async_computation.7 | async-start | bytes 4194304 | tf_op jit(solution)/shard_map/psum | solution.py:49
  661.1 289.3 %all-gather.5.cloned.1.call-start = ((), (), s32[]{:S(2)}) async-start(), calls=%async_computation.5 | async-start | bytes 5242880 | tf_op jit(solution)/shard_map/all_gather | solution.py:51
  769.7 2.7 copy-start.8
  950.5 8.1 copy-start.4
  950.5 8.1 copy-start.6
  958.6 17.1 %copy-start.1 = (f32[1024,440]{0,1:T(8,128)S(1)}, f32[1024,440]{0,1:T(8,128)}, u32[]{:S(2)}) copy-start(f32[1024,440]{0,1:T(8,128)} %param.8) | copy-start | bytes 5406724
Sparse Core Ops, SparseCore 0:
  14.0 136.6 all-reduce.10
  191.8 50.5 all-reduce.16
  245.5 44.4 reduce-scatter.2
  293.5 102.3 all-reduce.14
  545.2 33.7 all-gather.2
  616.6 44.4 reduce-scatter.4
  664.8 102.3 all-reduce.12
  916.7 33.7 all-gather.4
